TPU v7x, 256 devices: a whole 4x4x8 slice. The times are simulated.
256 devices in a mesh: rows: 128 (over x, y_hi, z, core), cols: 2 (over y_lo).
Axes of the slice: x: 4, y: 4 (y_hi: 2, y_lo: 2; y = y_hi * 2 + y_lo), z: 8, core: 2. Of those that a mesh axis runs over, the one named last changes fastest.
Arguments:
- ancestor: bfloat16 [24576, 24576], P('rows', 'cols'), may hold values from -6 to 6
- panel_below: bfloat16 [2048, 512], P('rows'), may hold values from -0.0625 to 0.0625
- panel_beside: bfloat16 [2048, 512], P('rows'), may hold values from -0.0625 to 0.0625
- inverse_lower: bfloat16 [512, 512], replicated, may hold values from -3 to 3
- inverse_upper: bfloat16 [512, 512], replicated, may hold values from -3 to 3
- list_below: int32 [16], replicated, may hold values from 0 to 191, as said below
- list_beside: int32 [16], replicated, may hold values from 0 to 191, as said below
- second_below: bfloat16 [2048, 512], P('rows'), may hold values from -0.0625 to 0.0625
- second_beside: bfloat16 [2048, 512], P('rows'), may hold values from -0.0625 to 0.0625
- linked_below: bfloat16 [512, 512], replicated, may hold values from -0.0625 to 0.0625
- linked_beside: bfloat16 [512, 512], replicated, may hold values from -0.0625 to 0.0625
- second_lower: bfloat16 [512, 512], replicated, may hold values from -3 to 3
- second_upper: bfloat16 [512, 512], replicated, may hold values from -3 to 3
- blocks_below: int32 [16], replicated, may hold values from 0 to 191, as said below
- blocks_beside: int32 [16], replicated, may hold values from 0 to 191, as said below
Outputs:
- new_lower: bfloat16 [24576, 512], P('rows', 'cols')
- new_upper: bfloat16 [24576, 512], P(('cols', 'rows'))
- new_diagonal: bfloat16 [512, 512], P(None, 'cols')
- next_lower: bfloat16 [24576, 512], P('rows', 'cols')
- next_upper: bfloat16 [24576, 512], P(('cols', 'rows'))
- next_link: bfloat16 [512, 512], replicated
- next_diagonal: bfloat16 [512, 512], P(None, 'cols')
Inputs may be any that keep to these rules, and one draw needn't show every extreme that they name: `list_below`: 16 distinct block numbers in ascending order; block 0 and block 191 are always listed. `list_beside`: 16 distinct block numbers in ascending order; block 0 and block 191 are always listed. `blocks_below`: 16 distinct block numbers in ascending order; block 0 and block 191 are always listed. `blocks_beside`: 16 distinct block numbers in ascending order; block 0 and block 191 are always listed.
All inputs are finite; a program needn't handle non-finite values.
Results may differ from a plain program's by a relative error of at most 0.0077.
Values may be sent and summed in bfloat16 or wider, within the bound.
A program may use at most 128 MiB of HBM per device.

v0:
```python
import jax
import jax.numpy as jnp
from jax import lax
from jax.sharding import PartitionSpec as P

BLK = 128


def normalise(panel, inverse):
    return jnp.dot(panel, inverse, preferred_element_type=jnp.float32).astype(jnp.bfloat16)


def normalise_by_rows(panel, inverse):
    return lax.dot_general(
        panel, inverse, (((1,), (1,)), ((), ())), preferred_element_type=jnp.float32
    ).astype(jnp.bfloat16)


def inner_rows(left, right):
    return lax.dot_general(
        left, right, (((0,), (0,)), ((), ())), preferred_element_type=jnp.float32
    )


def own_half(panel, first_column, half_width):
    return lax.dynamic_slice_in_dim(panel, first_column, half_width, 1)


def listed_columns(tile, blocks, first_block):
    block_count = tile.shape[1] // BLK
    local_ids = blocks - first_block
    inside = jnp.logical_and(local_ids >= 0, local_ids < block_count)
    picked = jnp.take(
        tile.reshape(tile.shape[0], block_count, BLK),
        jnp.clip(local_ids, 0, block_count - 1),
        axis=1,
    )
    return (picked.reshape(tile.shape[0], blocks.shape[0] * BLK), jnp.repeat(inside, BLK))


def masked_product(picked, inside, panel):
    kept = jnp.where(inside[:, None], panel, jnp.zeros_like(panel))
    return jnp.dot(picked, kept, preferred_element_type=jnp.float32)


def listed_rows(strips, blocks):
    shaped = strips.reshape(strips.shape[0] // BLK, BLK, strips.shape[1])
    return jnp.take(shaped, blocks, axis=0).reshape(blocks.shape[0] * BLK, strips.shape[1])


def rows_onto(panel, blocks, first_row, row_count):
    global_rows = first_row + jnp.arange(row_count, dtype=jnp.int32)
    block_of = global_rows // BLK
    offset = global_rows % BLK
    matches = block_of[:, None] == blocks[None, :]
    position = jnp.sum(
        jnp.where(matches, jnp.arange(blocks.shape[0], dtype=jnp.int32)[None, :], 0), axis=1
    )
    present = jnp.any(matches, axis=1)
    picked = jnp.take(panel, position * BLK + offset, axis=0)
    return jnp.where(present[:, None], picked, jnp.zeros_like(picked))


def lower_block(partial_value):
    return (-lax.psum_scatter(partial_value, "cols", scatter_dimension=1, tiled=True)).astype(
        jnp.bfloat16
    )


def diag_block(base_value, picked_rows, lower_local):
    summed = lax.psum(inner_rows(picked_rows, lower_local), "rows")
    return (base_value - summed).astype(jnp.bfloat16)


def body(
    ancestor,
    panel_below,
    panel_beside,
    inverse_lower,
    inverse_upper,
    list_below,
    list_beside,
    second_below,
    second_beside,
    linked_below,
    linked_beside,
    second_lower,
    second_upper,
    blocks_below,
    blocks_beside,
):
    row_devices = lax.axis_size("rows")
    row_at = lax.axis_index("rows")
    col_at = lax.axis_index("cols")
    col_devices = lax.axis_size("cols")
    tile_rows = ancestor.shape[0]
    tile_cols = ancestor.shape[1]
    width = inverse_lower.shape[0]
    half_width = width // col_devices
    first_column = col_at * half_width
    unit_below = normalise(panel_below, inverse_lower)
    unit_beside = normalise_by_rows(panel_beside, inverse_upper)
    below_next = normalise(second_below, second_lower)
    beside_next = normalise_by_rows(second_beside, second_upper)
    unit_below, unit_beside, below_next, beside_next = (
        lax.all_gather(unit_below, "rows", axis=0, tiled=True),
        lax.all_gather(unit_beside, "rows", axis=0, tiled=True),
        lax.all_gather(below_next, "rows", axis=0, tiled=True),
        lax.all_gather(beside_next, "rows", axis=0, tiled=True),
    )
    strips = lax.all_to_all(ancestor, "rows", split_axis=1, concat_axis=0, tiled=True)
    strip_width = tile_cols // row_devices
    strip_start = (col_at * row_devices + row_at) * strip_width
    first_block = col_at * (tile_cols // BLK)
    row_start = row_at * tile_rows
    picked, inside = listed_columns(ancestor, list_below, first_block)
    new_lower = lower_block(masked_product(picked, inside, unit_below))
    new_upper = (-inner_rows(listed_rows(strips, list_beside), unit_beside)).astype(jnp.bfloat16)
    base_first = jnp.dot(
        inverse_upper,
        own_half(inverse_lower, first_column, half_width),
        preferred_element_type=jnp.float32,
    )
    new_diagonal = diag_block(
        base_first, rows_onto(unit_beside, list_beside, row_start, tile_rows), new_lower
    )
    link_below = normalise(linked_below, second_lower)
    link_beside = normalise_by_rows(linked_beside, second_upper)
    link_rows = lax.dynamic_slice_in_dim(link_below, first_column, half_width, 0)
    picked_next, inside_next = listed_columns(ancestor, blocks_below, first_block)
    partial_value = masked_product(picked_next, inside_next, below_next) + jnp.dot(
        new_lower, link_rows, preferred_element_type=jnp.float32
    )
    next_lower = lower_block(partial_value)
    first_row = (row_at == 0).astype(jnp.float32)
    link_term = inner_rows(
        new_upper, rows_onto(below_next, blocks_below, strip_start, strip_width)
    ) + first_row * jnp.dot(new_diagonal, link_rows, preferred_element_type=jnp.float32)
    next_link = (-lax.psum(link_term, ("rows", "cols"))).astype(jnp.bfloat16)
    next_upper = (
        -(
            inner_rows(listed_rows(strips, blocks_beside), beside_next)
            + jnp.dot(new_upper, link_beside, preferred_element_type=jnp.float32)
        )
    ).astype(jnp.bfloat16)
    base_second = jnp.dot(
        second_upper,
        own_half(second_lower, first_column, half_width),
        preferred_element_type=jnp.float32,
    ) - inner_rows(link_beside, own_half(next_link, first_column, half_width))
    next_diagonal = diag_block(
        base_second, rows_onto(beside_next, blocks_beside, row_start, tile_rows), next_lower
    )
    return (new_lower, new_upper, new_diagonal, next_lower, next_upper, next_link, next_diagonal)


def solution(mesh):
    return jax.shard_map(
        body,
        mesh=mesh,
        in_specs=(
            P("rows", "cols"),
            P("rows", None),
            P("rows", None),
            P(),
            P(),
            P(),
            P(),
            P("rows", None),
            P("rows", None),
            P(),
            P(),
            P(),
            P(),
            P(),
            P(),
        ),
        out_specs=(
            P("rows", "cols"),
            P(("cols", "rows"), None),
            P(None, "cols"),
            P("rows", "cols"),
            P(("cols", "rows"), None),
            P(),
            P(None, "cols"),
        ),
        check_vma=False,
    )
```

profile of v0, /device:TPU:2, one launch (start us, length us, event | category | flops | bytes accessed | tf_op | source)
XLA Modules:
  0.0 2101.3 jit_solution(3499471611282957993)
XLA Ops:
  7.2 1.9 convolution_convert_fusion.4
  9.2 1.5 convolution_convert_fusion.2
  11.5 5.8 copy_bitcast_fusion
  17.3 3.0 gather_fusion.1
  20.4 110.8 %all-gather.5.cloned.1.call-done = bf16[2048,512]{1,0:T(8,128)(2,1)} async-done(((bf16[16,512]{1,0:T(8,128)(2,1)}), bf16[2048,512]{1,0:T(8,128)(2,1)}) %all-gather.5.cloned.1.call-update) | async-done | bytes 2097168 | tf_op jit(solution)/shard_map/all_gather | solution.py:106
  131.3 3.1 fusion.2
  135.3 10.1 all_to_all.12
  145.3 9.5 copy.76
  154.8 9.5 all-to-all-start
  165.4 3.0 gather_fusion.4
  169.3 86.8 %all-gather.9.cloned.1.call-done = bf16[2048,512]{1,0:T(8,128)(2,1)} async-done(((bf16[16,512]{1,0:T(8,128)(2,1)}), bf16[2048,512]{1,0:T(8,128)(2,1)}) %all-gather.9.cloned.1.call-update) | async-done | bytes 2097168 | tf_op jit(solution)/shard_map/all_gather | solution.py:108
  256.1 2.2 fusion
  258.3 20.8 reduce-scatter.3.cloned.1.call-done
  281.6 120.8 %all-gather.11.cloned.1.call-done = bf16[2048,512]{1,0:T(8,128)(2,1)} async-done(((bf16[16,512]{1,0:T(8,128)(2,1)}), bf16[2048,512]{1,0:T(8,128)(2,1)}) %all-gather.11.cloned.1.call-update) | async-done | bytes 2097168 | tf_op jit(solution)/shard_map/all_gather | solution.py:109
  402.4 2.9 gather_fusion.6
  405.3 114.1 %all-gather.7.cloned.1.call-done = bf16[2048,512]{1,0:T(8,128)(2,1)} async-done(((bf16[16,512]{1,0:T(8,128)(2,1)}), bf16[2048,512]{1,0:T(8,128)(2,1)}) %all-gather.7.cloned.1.call-update) | async-done | bytes 2097168 | tf_op jit(solution)/shard_map/all_gather | solution.py:107
  519.4 2.9 gather_fusion.3
  523.5 13.4 reduce-scatter.5.cloned.1.call-done
  542.3 3.3 gather_fusion
  545.6 1206.7 %all-reduce.6.cloned.1.call-done = (f32[512,256]{0,1:T(8,128)}, f32[512,256]{0,1:T(8,128)}) async-done(((f32[512,256]{0,1:T(8,128)}, f32[512,256]{0,1:T(8,128)}), (f32[512,256]{0,1:T(8,128)}, f32[512,256]{0,1:T(8,128)})) %all-reduce.6.cloned.1.call-update) | async-done | bytes 1048592 | tf_op jit(solution)/shard_map/psum | solution.py:71
  1755.9 8.2 copy.78
  1764.1 3.0 gather_fusion.2
  1770.4 3.0 gather_fusion.5
  1775.1 315.4 %all-reduce.4.cloned.1.call-done = f32[512,512]{1,0:T(8,128)} async-done(((f32[512,512]{1,0:T(8,128)}), f32[512,512]{1,0:T(8,128)}) %all-reduce.4.cloned.1.call-update) | async-done | bytes 1048592 | tf_op jit(solution)/shard_map/psum | solution.py:139
  (102 shorter events, 25.0 us)
Async XLA Ops:
  7.2 2.0 copy-start
  7.2 124.1 %all-gather.5.cloned.1.call-start = ((), (), s32[]{:S(2)}) async-start(), calls=%async_computation.3 | async-start | bytes 2113536 | tf_op jit(solution)/shard_map/all_gather | solution.py:106
  9.2 246.9 %all-gather.9.cloned.1.call-start = ((), (), s32[]{:S(2)}) async-start(), calls=%async_computation.6 | async-start | bytes 2113536 | tf_op jit(solution)/shard_map/all_gather | solution.py:108
  10.7 268.4 %reduce-scatter.3.cloned.1.call-start = ((), (), s32[]{:S(2)}) async-start(), calls=%async_computation.4 | async-start | bytes 589824 | tf_op jit(solution)/shard_map/reduce_scatter | solution.py:65
  131.2 3.1 copy-start.2
  131.2 3.1 copy-start.15
  134.3 268.1 %all-gather.11.cloned.1.call-start = ((), (), s32[]{:S(2)}) async-start(), calls=%async_computation.8 | async-start | bytes 2113536 | tf_op jit(solution)/shard_map/all_gather | solution.py:109
  154.8 9.6 copy-start.5
  154.8 9.6 copy-start.16
  154.8 1601.1 %all-to-all-start = ((bf16[192,128,96]{2,0,1:T(8,128)(2,1)}), bf16[192,128,96]{2,0,1:T(8,128)(2,1)}, u32[]{:S(2)}, u32[]{:S(2)}) async-start(bf16[192,128,96]{2,0,1:T(8,128)(2,1)} %copy.76), calls=%async_computation.1 | async-start | bytes 12582912 | tf_op jit(solution)/shard_map/all_to_all | solution.py:111
  164.3 4.2 copy-start.17
  164.3 4.2 copy-start.18
  164.3 4.3 copy-start.19
  164.3 4.5 copy-start.10
  164.3 355.1 %all-gather.7.cloned.1.call-start = ((), (), s32[]{:S(2)}) async-start(), calls=%async_computation.5 | async-start | bytes 2113536 | tf_op jit(solution)/shard_map/all_gather | solution.py:107
  165.3 371.6 %reduce-scatter.5.cloned.1.call-start = ((), (), s32[]{:S(2)}) async-start(), calls=%async_computation.7 | async-start | bytes 589824 | tf_op jit(solution)/shard_map/reduce_scatter | solution.py:65
  280.1 242.2 %copy-start.9 = (bf16[192,256]{1,0:T(8,128)(2,1)}, bf16[192,256]{1,0:T(8,128)(2,1)S(1)}, u32[]{:S(2)}) copy-start(bf16[192,256]{1,0:T(8,128)(2,1)S(1)} %negate_convert_fusion.2) | copy-start | bytes 294916
  281.1 1471.2 %all-reduce.6.cloned.1.call-start = ((), (), s32[]{:S(2)}) async-start(), calls=%async_computation.10 | async-start | bytes 2097152 | tf_op jit(solution)/shard_map/psum | solution.py:71
  538.5 1213.9 %copy-start.8 = (bf16[512,512]{1,0:T(8,128)(2,1)S(1)}, bf16[512,512]{1,0:T(8,128)(2,1)}, u32[]{:S(2)}) copy-start(bf16[512,512]{1,0:T(8,128)(2,1)} %param.24) | copy-start | bytes 1572868
  539.7 1550.8 %all-reduce.4.cloned.1.call-start = ((), (), s32[]{:S(2)}) async-start(), calls=%async_computation.9 | async-start | bytes 2097152 | tf_op jit(solution)/shard_map/psum | solution.py:139
  1755.9 11.2 copy-start.7
  1769.0 4.3 copy-start.1
  1774.3 318.0 %copy-start.3 = (bf16[512,512]{1,0:T(8,128)(2,1)S(1)}, bf16[512,512]{1,0:T(8,128)(2,1)}, u32[]{:S(2)}) copy-start(bf16[512,512]{1,0:T(8,128)(2,1)} %param.33) | copy-start | bytes 1572868
  2091.8 2.6 copy-start.6
  (6 other events, 8.0 us)
Sparse Core Ops, SparseCore 0:
  12.3 118.9 all-gather.4
  135.5 120.4 all-gather.8
  259.2 19.9 reduce-scatter.2
  283.3 119.0 all-gather.10
  406.5 112.8 all-gather.6
  521.7 15.1 reduce-scatter.4
  540.1 1212.1 all-reduce.5
  1770.5 319.9 all-reduce.3
where the time goes:
time: 2100 us
  waiting for transfers between devices  1990 us (95%)
  local copies, waits for them, and re-layouts  58.2 us (3%)
  matrix products  24.1 us (1%)
    psum x1, waiting for transfers between devices, diag_block(): summed = lax.psum(inner_rows(picked_rows, lower_local), 'rows')  1210 us
    psum x1, waiting for transfers between devices, body(): next_link = (-lax.psum(link_term, ('rows', 'cols'))).astype(jnp.bfloat16)  315 us
    all_gather x1, waiting for transfers between devices, body(): lax.all_gather(beside_next, 'rows', axis=0, tiled=True)  121 us
    all_gather x1, waiting for transfers between devices, body(): lax.all_gather(unit_beside, 'rows', axis=0, tiled=True)  114 us
    all_gather x1, waiting for transfers between devices, body(): lax.all_gather(unit_below, 'rows', axis=0, tiled=True)  111 us
    all_gather x1, waiting for transfers between devices, body(): lax.all_gather(below_next, 'rows', axis=0, tiled=True)  86.8 us
  transfers between devices with their start and end apart: 9, of which 8 were waited for; matrix products, arithmetic and copies ran while one was open for 3% of the time, Pallas kernels for 0%

commit v1 on v0

--- a/solution.py
+++ b/solution.py
@@ -103,7 +103,9 @@
     below_next = normalise(second_below, second_lower)
     beside_next = normalise_by_rows(second_beside, second_upper)
     unit_below, unit_beside, below_next, beside_next = (
-        lax.all_gather(unit_below, "rows", axis=0, tiled=True),
+        jnp.concatenate(
+            lax.all_to_all(jnp.stack([unit_below] * lax.axis_size("rows")), "rows", 0, 0), axis=0
+        ),
         lax.all_gather(unit_beside, "rows", axis=0, tiled=True),
         lax.all_gather(below_next, "rows", axis=0, tiled=True),
         lax.all_gather(beside_next, "rows", axis=0, tiled=True),

time: 2100 us -> 1970 us (0.938)
  waiting for transfers between devices: 1990 us -> 1840 us
    all_gather x1 -> x0, waiting for transfers between devices: 111 us -> none  [body(): lax.all_gather(unit_below, 'rows', axis=0, tiled=True)]
    all_to_all x0 -> x1, waiting for transfers between devices: none -> 41.1 us  [body(): lax.all_to_all(jnp.stack([unit_below] * lax.axis_size('rows')), 'rows', 0...]
    all_gather x1, waiting for transfers between devices: 86.8 us -> 48.1 us  [body(): lax.all_gather(below_next, 'rows', axis=0, tiled=True)]
    reduce_scatter x2, waiting for transfers between devices: 34.3 us -> 0.03 us  [lower_block(): lax.psum_scatter(partial_value, 'cols', scatter_dimension=1, tiled=True)]
  transfers between devices with their start and end apart: 9 -> 9, of which waited for: 8 -> 6; matrix products, arithmetic and copies ran while one was open for 3% -> 3% of each run, Pallas kernels for 0% -> 0%
where the time goes in v1:
time: 1970 us
  waiting for transfers between devices  1840 us (93%)
  local copies, waits for them, and re-layouts  59.9 us (3%)
  starting transfers between devices  26.2 us (1%)
  matrix products  21.1 us (1%)
    psum x1, waiting for transfers between devices, diag_block(): summed = lax.psum(inner_rows(picked_rows, lower_local), 'rows')  1200 us
    psum x1, waiting for transfers between devices, body(): next_link = (-lax.psum(link_term, ('rows', 'cols'))).astype(jnp.bfloat16)  315 us
    all_gather x1, waiting for transfers between devices, body(): lax.all_gather(beside_next, 'rows', axis=0, tiled=True)  120 us
    all_gather x1, waiting for transfers between devices, body(): lax.all_gather(unit_beside, 'rows', axis=0, tiled=True)  114 us
    all_gather x1, waiting for transfers between devices, body(): lax.all_gather(below_next, 'rows', axis=0, tiled=True)  48.1 us
    all_to_all x1, waiting for transfers between devices, body(): lax.all_to_all(jnp.stack([unit_below] * lax.axis_size('rows')), 'rows', 0...  41.1 us
  transfers between devices with their start and end apart: 9, of which 6 were waited for; matrix products, arithmetic and copies ran while one was open for 3% of the time, Pallas kernels for 0%

profile of v1, /device:TPU:2, one launch (start us, length us, event | category | flops | bytes accessed | tf_op | source)
XLA Modules:
  0.0 1968.9 jit_solution(14450077130000370067)
XLA Ops:
  9.3 1.6 stack.2
  10.9 15.7 all-to-all-start
  27.8 5.8 copy_bitcast_fusion
  33.5 3.0 gather_fusion.1
  36.6 41.1 %all-to-all-done = bf16[128,16,512]{2,1,0:T(8,128)(2,1)S(1)} async-done(((bf16[128,16,512]{2,1,0:T(8,128)(2,1)}), bf16[128,16,512]{2,1,0:T(8,128)(2,1)S(1)}, u32[]{:S(2)}, u32[]{:S(2)}) %all-to-all-start) | async-done | bytes 2097184 | tf_op jit(solution)/shard_map/all_to_all | solution.py:107
  80.3 10.1 all_to_all.16
  90.4 9.5 copy.76
  99.9 10.1 all-to-all-start.1
  111.2 3.0 gather_fusion.4
  115.1 48.1 %all-gather.6.cloned.1.call-done = bf16[2048,512]{1,0:T(8,128)(2,1)} async-done(((bf16[16,512]{1,0:T(8,128)(2,1)}), bf16[2048,512]{1,0:T(8,128)(2,1)}) %all-gather.6.cloned.1.call-update) | async-done | bytes 2097168 | tf_op jit(solution)/shard_map/all_gather | solution.py:110
  163.2 2.2 fusion
  167.7 119.9 %all-gather.8.cloned.1.call-done = bf16[2048,512]{1,0:T(8,128)(2,1)} async-done(((bf16[16,512]{1,0:T(8,128)(2,1)}), bf16[2048,512]{1,0:T(8,128)(2,1)}) %all-gather.8.cloned.1.call-update) | async-done | bytes 2097168 | tf_op jit(solution)/shard_map/all_gather | solution.py:111
  287.6 2.9 gather_fusion.6
  290.5 114.3 %all-gather.4.cloned.1.call-done = bf16[2048,512]{1,0:T(8,128)(2,1)} async-done(((bf16[16,512]{1,0:T(8,128)(2,1)}), bf16[2048,512]{1,0:T(8,128)(2,1)}) %all-gather.4.cloned.1.call-update) | async-done | bytes 2097168 | tf_op jit(solution)/shard_map/all_gather | solution.py:109
  404.7 2.9 gather_fusion.3
  412.7 1.5 convolution_convert_fusion
  414.2 3.3 gather_fusion
  417.5 1202.2 %all-reduce.6.cloned.1.call-done = (f32[512,256]{0,1:T(8,128)}, f32[512,256]{0,1:T(8,128)}) async-done(((f32[512,256]{0,1:T(8,128)}, f32[512,256]{0,1:T(8,128)}), (f32[512,256]{0,1:T(8,128)}, f32[512,256]{0,1:T(8,128)})) %all-reduce.6.cloned.1.call-update) | async-done | bytes 1048592 | tf_op jit(solution)/shard_map/psum | solution.py:71
  1619.7 1.4 fusion.7
  1623.3 8.2 copy.78
  1631.5 3.0 gather_fusion.2
  1637.8 3.0 gather_fusion.5
  1642.5 315.1 %all-reduce.4.cloned.1.call-done = f32[512,512]{1,0:T(8,128)} async-done(((f32[512,512]{1,0:T(8,128)}), f32[512,512]{1,0:T(8,128)}) %all-reduce.4.cloned.1.call-update) | async-done | bytes 1048592 | tf_op jit(solution)/shard_map/psum | solution.py:141
  1959.3 1.4 fusion.6
  (108 shorter events, 23.8 us)
Async XLA Ops:
  8.0 18.6 copy-start
  10.9 15.7 copy-start.15
  10.9 16.6 copy-start.20
  10.9 16.6 copy-start.21
  10.9 66.8 %all-to-all-start = ((bf16[128,16,512]{2,1,0:T(8,128)(2,1)}), bf16[128,16,512]{2,1,0:T(8,128)(2,1)S(1)}, u32[]{:S(2)}, u32[]{:S(2)}) async-start(bf16[128,16,512]{2,1,0:T(8,128)(2,1)} %stack.2), calls=%async_computation | async-start | bytes 4194304 | tf_op jit(solution)/shard_map/all_to_all | solution.py:107
  26.6 136.6 %all-gather.6.cloned.1.call-start = ((), (), s32[]{:S(2)}) async-start(), calls=%async_computation.6 | async-start | bytes 2113536 | tf_op jit(solution)/shard_map/all_gather | solution.py:110
  27.5 138.0 %reduce-scatter.3.cloned.1.call-start = ((), (), s32[]{:S(2)}) async-start(), calls=%async_computation.4 | async-start | bytes 589824 | tf_op jit(solution)/shard_map/reduce_scatter | solution.py:65
  79.4 208.2 %all-gather.8.cloned.1.call-start = ((), (), s32[]{:S(2)}) async-start(), calls=%async_computation.8 | async-start | bytes 2113536 | tf_op jit(solution)/shard_map/all_gather | solution.py:111
  99.9 10.2 copy-start.5
  99.9 10.2 copy-start.17
  99.9 1523.4 %all-to-all-start.1 = ((bf16[192,128,96]{2,0,1:T(8,128)(2,1)}), bf16[192,128,96]{2,0,1:T(8,128)(2,1)}, u32[]{:S(2)}, u32[]{:S(2)}) async-start(bf16[192,128,96]{2,0,1:T(8,128)(2,1)} %copy.76), calls=%async_computation.2 | async-start | bytes 12582912 | tf_op jit(solution)/shard_map/all_to_all | solution.py:113
  109.9 4.3 copy-start.18
  109.9 4.3 copy-start.19
  110.0 4.7 copy-start.10
  110.0 294.8 %all-gather.4.cloned.1.call-start = ((), (), s32[]{:S(2)}) async-start(), calls=%async_computation.5 | async-start | bytes 2113536 | tf_op jit(solution)/shard_map/all_gather | solution.py:109
  110.9 297.9 %reduce-scatter.5.cloned.1.call-start = ((), (), s32[]{:S(2)}) async-start(), calls=%async_computation.7 | async-start | bytes 589824 | tf_op jit(solution)/shard_map/reduce_scatter | solution.py:65
  166.4 241.2 %copy-start.9 = (bf16[192,256]{1,0:T(8,128)(2,1)}, bf16[192,256]{1,0:T(8,128)(2,1)S(1)}, u32[]{:S(2)}) copy-start(bf16[192,256]{1,0:T(8,128)(2,1)S(1)} %negate_convert_fusion.2) | copy-start | bytes 294916
  167.4 1452.3 %all-reduce.6.cloned.1.call-start = ((), (), s32[]{:S(2)}) async-start(), calls=%async_computation.10 | async-start | bytes 2097152 | tf_op jit(solution)/shard_map/psum | solution.py:71
  410.4 1209.4 %copy-start.8 = (bf16[512,512]{1,0:T(8,128)(2,1)S(1)}, bf16[512,512]{1,0:T(8,128)(2,1)}, u32[]{:S(2)}) copy-start(bf16[512,512]{1,0:T(8,128)(2,1)} %param.24) | copy-start | bytes 1572868
  411.6 1546.0 %all-reduce.4.cloned.1.call-start = ((), (), s32[]{:S(2)}) async-start(), calls=%async_computation.9 | async-start | bytes 2097152 | tf_op jit(solution)/shard_map/psum | solution.py:141
  1623.3 11.2 copy-start.7
  1636.4 4.3 copy-start.1
  1641.7 317.6 %copy-start.3 = (bf16[512,512]{1,0:T(8,128)(2,1)S(1)}, bf16[512,512]{1,0:T(8,128)(2,1)}, u32[]{:S(2)}) copy-start(bf16[512,512]{1,0:T(8,128)(2,1)} %param.33) | copy-start | bytes 1572868
  1958.9 2.6 copy-start.6
  (8 other events, 11.0 us)
Sparse Core Ops, SparseCore 0:
  31.7 131.4 all-gather.5
  167.5 120.0 all-gather.7
  291.9 112.8 all-gather.3
  411.7 1208.0 all-reduce.5
Sparse Core Ops, SparseCore 1:
  79.5 15.1 reduce-scatter.2
  167.5 17.3 reduce-scatter.4
  1637.9 319.7 all-reduce.3
